TPU v7x, 512 devices: a whole 4x8x8 slice. The times are simulated.
512 devices in a mesh: dp: 16 (over x, y_hi), dom: 32 (over z, y_lo, core).
Axes of the slice: x: 4, y: 8 (y_hi: 4, y_lo: 2; y = y_hi * 2 + y_lo), z: 8, core: 2. Of those that a mesh axis runs over, the one named last changes fastest.
Arguments:
- features: bfloat16 [16, 16384, 128], P('dp', 'dom'), may hold values from -6 to 6
- keep_masks: bfloat16 [16, 4, 16384], P('dp', None, 'dom'), may hold values from 0 to 1, as said below
- serve_ids: int32 [16, 32, 32, 1], P('dp', 'dom'), may hold values from 0 to 3, as said below
- col_slot: int32 [16, 128, 10], P('dp', 'dom'), may hold values from 0 to 35, as said below
- adj_blocks: bfloat16 [16, 128, 10, 128, 128], P('dp', 'dom'), may hold values from -0.15625 to 0.15625
- node_labels: int32 [16, 16384], P('dp', 'dom'), may hold values from 0 to 171
- labeled: int32 [16, 16384], P('dp', 'dom'), may hold values 0 or 1
- weight_in: bfloat16 [128, 1024], replicated, may hold values from -0.5 to 0.5
- bias_in: float32 [1024], replicated, may hold values from -3 to 3
- weight_out: bfloat16 [1024, 172], replicated, may hold values from -0.1875 to 0.1875
- bias_out: float32 [172], replicated, may hold values from -4 to 4
Outputs:
- grad_weight_in: float32 [128, 1024], replicated
- grad_bias_in: float32 [1024], replicated
- grad_weight_out: float32 [1024, 172], replicated
- grad_bias_out: float32 [172], replicated
Inputs may be any that keep to these rules, and one draw needn't show every extreme that they name: `serve_ids`: for each batch, sending device and receiving device: 1 distinct own tile numbers of the sender. `col_slot`: slots below 32 name received tiles; within one device's row tiles every such slot is named exactly once and each own tile slot exactly 2 times. `keep_masks`: values are 0 or 1.
All inputs are finite; a program needn't handle non-finite values. No bound on the sum of `labeled` on one device may be relied on, other than what follows from the above.
Results may differ from a plain program's by a relative error of at most 0.0015.
Values may be sent and summed in bfloat16 or wider, within the bound.
A program may use at most 64 MiB of HBM per device.

v0:
```python
import jax
import jax.numpy as jnp
from jax import lax
from jax.sharding import PartitionSpec as P

ORDER = 2
KEEP_RATE = 0.5


def tile_products(block_vals, picked):
    return jnp.einsum("rjab,rjsbf->rsaf", block_vals, picked, preferred_element_type=jnp.float32)


def mlp_grads(xbar, node_labels, labeled, weight_in, bias_in, weight_out, bias_out, scale):
    row_tiles, samples, tile_size, feat_size = xbar.shape
    classes = weight_out.shape[1]
    node_rows = xbar.reshape(-1, feat_size)
    hidden_pre = jnp.dot(node_rows, weight_in, preferred_element_type=jnp.float32) + bias_in
    activation = jax.nn.silu(hidden_pre).astype(jnp.bfloat16)
    logits = jnp.dot(activation, weight_out, preferred_element_type=jnp.float32) + bias_out
    expo = jnp.exp(logits)
    prob = (expo / jnp.sum(expo, -1, keepdims=True)).reshape(row_tiles, samples, tile_size, classes)
    average = jnp.mean(prob, axis=1)
    squares = average * average
    sharp = squares / jnp.sum(squares, -1, keepdims=True)
    onehot = (
        node_labels.reshape(row_tiles, tile_size)[..., None] == jnp.arange(classes, dtype=jnp.int32)
    ).astype(jnp.float32)
    used = labeled.reshape(row_tiles, 1, tile_size, 1).astype(jnp.float32)
    push = 2.0 * (prob - sharp[:, None])
    inner = jnp.sum(push * prob, -1, keepdims=True)
    dlogits = (used * (prob - onehot[:, None]) + prob * (push - inner)) * scale
    dlogits = dlogits.reshape(-1, classes)
    dlog_b = dlogits.astype(jnp.bfloat16)
    grad_weight_out = jnp.dot(activation.T, dlog_b, preferred_element_type=jnp.float32)
    grad_bias_out = jnp.sum(dlogits, 0)
    dact = jnp.dot(dlog_b, weight_out.T, preferred_element_type=jnp.float32)
    sigma = jax.nn.sigmoid(hidden_pre)
    dpre = dact * sigma * (1.0 + hidden_pre * (1.0 - sigma))
    grad_bias_in = jnp.sum(dpre, 0)
    grad_weight_in = jnp.dot(
        node_rows.T, dpre.astype(jnp.bfloat16), preferred_element_type=jnp.float32
    )
    return (grad_weight_in, grad_bias_in, grad_weight_out, grad_bias_out)


def per_device(
    features,
    keep_masks,
    serve_ids,
    col_slot,
    adj_blocks,
    node_labels,
    labeled,
    weight_in,
    bias_in,
    weight_out,
    bias_out,
):
    tiles_dev = col_slot.shape[1]
    tile_size = adj_blocks.shape[-1]
    feat_size = features.shape[-1]
    samples = keep_masks.shape[1]
    dom_count = lax.axis_size("dom")
    capacity = serve_ids.shape[-1]
    send_ids = serve_ids[0, 0].reshape(-1)
    slot_ids = col_slot[0]
    block_vals = adj_blocks[0]
    own_tiles = features[0].reshape(tiles_dev, tile_size, feat_size)
    mask_tiles = keep_masks[0].reshape(samples, tiles_dev, tile_size).transpose(1, 0, 2)
    masked = mask_tiles[:, :, :, None] * own_tiles[:, None, :, :]
    outgoing = masked[send_ids].reshape(dom_count, capacity, samples, tile_size, feat_size)
    incoming = lax.all_to_all(outgoing, "dom", split_axis=0, concat_axis=0, tiled=True)
    pool = jnp.concatenate([incoming.reshape(-1, samples, tile_size, feat_size), masked], 0)
    picked = pool[slot_ids]
    result = tile_products(block_vals, picked)
    total = masked.astype(jnp.float32) + result
    current = result.astype(jnp.bfloat16)
    outgoing = current[send_ids].reshape(dom_count, capacity, samples, tile_size, feat_size)
    incoming = lax.all_to_all(outgoing, "dom", split_axis=0, concat_axis=0, tiled=True)
    pool = jnp.concatenate([incoming.reshape(-1, samples, tile_size, feat_size), current], 0)
    result = tile_products(block_vals, pool[slot_ids])
    total = total + result
    xbar = (total * (1.0 / ((ORDER + 1) * KEEP_RATE))).astype(jnp.bfloat16)
    scale = 1.0 / (samples * tiles_dev * tile_size)
    grad_w1, grad_b1, grad_w2, grad_b2 = mlp_grads(
        xbar, node_labels[0], labeled[0], weight_in, bias_in, weight_out, bias_out, scale
    )
    grad_w1, grad_b1, grad_w2, grad_b2 = lax.psum(
        (grad_w1, grad_b1, grad_w2, grad_b2), ("dp", "dom")
    )
    return (grad_w1, grad_b1, grad_w2, grad_b2)


def solution(mesh):
    placed = (
        P("dp", "dom", None),
        P("dp", None, "dom"),
        P("dp", "dom", None, None),
        P("dp", "dom", None),
        P("dp", "dom", None, None, None),
        P("dp", "dom"),
        P("dp", "dom"),
        P(),
        P(),
        P(),
        P(),
    )
    return jax.shard_map(
        per_device, mesh=mesh, in_specs=placed, out_specs=(P(), P(), P(), P()), check_vma=False
    )
```

profile of v0, /device:TPU:17, one launch (start us, length us, event | category | flops | bytes accessed | tf_op | source)
XLA Modules:
  0.0 595.5 jit_solution(16002134750879423810)
XLA Ops:
  7.2 0.0 copy-start
  7.2 0.8 fusion.20
  8.0 1.2 broadcast_multiply_fusion
  9.2 3.1 gather_fusion
  12.3 12.3 %all-to-all-start = ((bf16[32,1,4,128,128]{4,3,2,1,0:T(8,128)(2,1)}), bf16[32,1,4,128,128]{4,3,2,1,0:T(8,128)(2,1)}, u32[]{:S(2)}, u32[]{:S(2)}) async-start(bf16[32,1,4,128,128]{4,3,2,1,0:T(8,128)(2,1)} %bitcast.86), calls=%async_computation | async-start | bytes 8388608 | tf_op jit(solution)/shard_map/all_to_all | solution.py:73
  24.6 0.0 copy-done.6
  24.6 0.1 reshape.132
  24.7 101.8 %all-to-all-done = bf16[32,1,4,128,128]{4,3,2,1,0:T(8,128)(2,1)} async-done(((bf16[32,1,4,128,128]{4,3,2,1,0:T(8,128)(2,1)}), bf16[32,1,4,128,128]{4,3,2,1,0:T(8,128)(2,1)}, u32[]{:S(2)}, u32[]{:S(2)}) %all-to-all-start) | async-done | bytes 4194336 | tf_op jit(solution)/shard_map/all_to_all | solution.py:73
  126.5 4.8 pad_maximum_fusion
  131.3 6.9 %gather_fusion.1 = bf16[40,4,128,128]{3,2,1,0:T(8,128)(2,1)} fusion(bf16[36,4,128,128]{3,2,1,0:T(8,128)(2,1)} %pad_maximum_fusion, s32[1024]{0:T(1024)S(1)} %pad_clamp_fusion), kind=kCustom, calls=%fused_computation.1 | custom fusion | bytes 10485920 | tf_op jit(solution)/shard_map/gather | solution.py:75
  138.2 0.0 copy-done
  138.2 4.4 fusion.22
  142.7 3.1 gather_fusion.2
  145.7 9.6 %all-to-all-start.1 = ((bf16[32,1,4,128,128]{4,3,2,1,0:T(8,128)(2,1)}), bf16[32,1,4,128,128]{4,3,2,1,0:T(8,128)(2,1)}, u32[]{:S(2)}, u32[]{:S(2)}) async-start(bf16[32,1,4,128,128]{4,3,2,1,0:T(8,128)(2,1)} %bitcast.85), calls=%async_computation.1 | async-start | bytes 8388608 | tf_op jit(solution)/shard_map/all_to_all | solution.py:80
  155.4 0.0 all-reduce.4.cloned.1.call-start
  155.4 0.0 copy-done.7
  155.5 0.0 copy-done.5
  155.5 0.1 fusion.17
  155.6 0.2 sub.35
  155.8 1.7 sub.36
  157.5 99.8 %all-to-all-done.1 = bf16[32,1,4,128,128]{4,3,2,1,0:T(8,128)(2,1)} async-done(((bf16[32,1,4,128,128]{4,3,2,1,0:T(8,128)(2,1)}), bf16[32,1,4,128,128]{4,3,2,1,0:T(8,128)(2,1)}, u32[]{:S(2)}, u32[]{:S(2)}) %all-to-all-start.1) | async-done | bytes 4194336 | tf_op jit(solution)/shard_map/all_to_all | solution.py:80
  257.3 4.8 pad_maximum_fusion.1
  262.1 7.2 %gather_fusion.3 = bf16[40,4,128,128]{3,2,1,0:T(8,128)(2,1)} fusion(bf16[36,4,128,128]{3,2,1,0:T(8,128)(2,1)} %pad_maximum_fusion.1, s32[1024]{0:T(1024)S(1)} %pad_clamp_fusion), kind=kCustom, calls=%fused_computation.3 | custom fusion | bytes 10485920 | tf_op jit(solution)/shard_map/gather | solution.py:82
  269.3 3.6 fusion.11
  272.9 0.0 copy-start.8
  272.9 0.0 copy-start.11
  272.9 4.6 multiply_convert_fusion
  277.6 1.6 fusion.23
  279.2 0.3 copy-done.12
  279.5 1.3 broadcast_divide_fusion
  280.8 3.0 reshape.121
  283.8 2.3 reduce_sum.55
  286.1 0.2 fusion.19
  286.3 0.1 fusion.18
  286.4 1.3 sub.38
  287.7 2.8 sub.39
  290.5 1.8 multiply_reduce_fusion
  292.3 2.5 fusion.21
  294.7 1.8 fusion.14
  296.5 6.5 %fusion.24 = (f32[1024]{0:T(1024)S(1)}, bf16[2048,1024]{1,0:T(8,128)(2,1)S(1)}) fusion(f32[2048,1024]{1,0:T(8,128)} %get-tuple-element.13, f32[1024]{0:T(1024)S(1)} %copy-done.10, bf16[1024,172]{0,1:T(8,128)(2,1)S(1)} %copy-done.8, bf16[2048,172]{0,1:T(8,128)(2,1)S(1)} %get-tuple-element.9), kind=kOutput, calls=%fused_computation.41 | convolution fusion | flops 744487936 | bytes 13647872 | tf_op jit(solution)/shard_map/dot_general | solution.py:37
  303.0 0.0 copy-start.1
  303.0 1.6 fusion
  304.6 0.0 all-reduce.4.cloned.1.call-update
  304.6 99.8 %all-reduce = (f32[1024]{0:T(1024)}, f32[172]{0:T(256)}) all-reduce(f32[1024]{0:T(1024)S(1)} %get-tuple-element.16, f32[172]{0:T(256)S(1)} %get-tuple-element.8), channel_id=1, replica_groups=mesh['dp'=16,'dom'=32] {'dp','dom'}, use_global_device_ids=true, to_apply=%region_6.7 | all-reduce | flops 1196 | bytes 9568 | tf_op jit(solution)/shard_map/psum | solution.py:89
  404.4 180.3 %all-reduce.4.cloned.1.call-done = (f32[128,1024]{1,0:T(8,128)}, f32[1024,172]{0,1:T(8,128)}) async-done(((f32[128,1024]{1,0:T(8,128)}, f32[1024,172]{0,1:T(8,128)}), (f32[128,1024]{1,0:T(8,128)}, f32[1024,172]{0,1:T(8,128)})) %all-reduce.4.cloned.1.call-update) | async-done | bytes 1228816 | tf_op jit(solution)/shard_map/psum | solution.py:89
  584.8 1.9 copy.28
  586.7 2.0 copy.29
  588.7 0.0 copy-done.1
  (23 shorter events, 0.1 us)
Async XLA Ops:
  7.2 131.1 %copy-start = (bf16[1,4,10,128,128]{4,3,2,1,0:T(8,128)(2,1)S(1)}, bf16[1,4,10,128,128]{4,3,2,1,0:T(8,128)(2,1)}, u32[]{:S(2)}) copy-start(bf16[1,4,10,128,128]{4,3,2,1,0:T(8,128)(2,1)} %param.15) | copy-start | bytes 3932164
  12.3 12.4 %copy-start.6 = (s32[1,4,10]{2,1,0:T(4,128)S(1)}, s32[1,4,10]{2,1,0:T(4,128)}, u32[]{:S(2)}) copy-start(s32[1,4,10]{2,1,0:T(4,128)} %param.14) | copy-start | bytes 484
  12.3 114.3 %all-to-all-start = ((bf16[32,1,4,128,128]{4,3,2,1,0:T(8,128)(2,1)}), bf16[32,1,4,128,128]{4,3,2,1,0:T(8,128)(2,1)}, u32[]{:S(2)}, u32[]{:S(2)}) async-start(bf16[32,1,4,128,128]{4,3,2,1,0:T(8,128)(2,1)} %bitcast.86), calls=%async_computation | async-start | bytes 8388608 | tf_op jit(solution)/shard_map/all_to_all | solution.py:73
  145.7 9.7 %copy-start.7 = (s32[1,512]{1,0:T(1,128)S(1)}, s32[1,512]{1,0:T(1,128)}, u32[]{:S(2)}) copy-start(s32[1,512]{1,0:T(1,128)} %param.17) | copy-start | bytes 6148
  145.7 9.7 %copy-start.5 = (s32[1,512]{1,0:T(1,128)S(1)}, s32[1,512]{1,0:T(1,128)}, u32[]{:S(2)}) copy-start(s32[1,512]{1,0:T(1,128)} %param.16) | copy-start | bytes 6148
  145.7 111.6 %all-to-all-start.1 = ((bf16[32,1,4,128,128]{4,3,2,1,0:T(8,128)(2,1)}), bf16[32,1,4,128,128]{4,3,2,1,0:T(8,128)(2,1)}, u32[]{:S(2)}, u32[]{:S(2)}) async-start(bf16[32,1,4,128,128]{4,3,2,1,0:T(8,128)(2,1)} %bitcast.85), calls=%async_computation.1 | async-start | bytes 8388608 | tf_op jit(solution)/shard_map/all_to_all | solution.py:80
  155.4 429.4 %all-reduce.4.cloned.1.call-start = ((), (), s32[]{:S(2)}) async-start(), calls=%async_computation.2 | async-start | bytes 2490368 | tf_op jit(solution)/shard_map/psum | solution.py:89
  262.1 7.2 %copy-start.2 = (f32[4,4,128,128]{3,2,1,0:T(8,128)S(1)}, f32[4,4,128,128]{3,2,1,0:T(8,128)}, u32[]{:S(2)}) copy-start(f32[4,4,128,128]{3,2,1,0:T(8,128)} %get-tuple-element.11) | copy-start | bytes 3145732
  262.1 7.2 %copy-start.3 = (bf16[1,512,128]{2,1,0:T(8,128)(2,1)S(1)}, bf16[1,512,128]{2,1,0:T(8,128)(2,1)}, u32[]{:S(2)}) copy-start(bf16[1,512,128]{2,1,0:T(8,128)(2,1)} %param.11) | copy-start | bytes 393220
  262.1 7.2 %copy-start.4 = (bf16[1,4,512]{2,1,0:T(4,128)(2,1)S(1)}, bf16[1,4,512]{2,1,0:T(4,128)(2,1)}, u32[]{:S(2)}) copy-start(bf16[1,4,512]{2,1,0:T(4,128)(2,1)} %param.12) | copy-start | bytes 12292
  269.3 3.6 copy-start.9
  269.3 3.6 copy-start.10
  272.9 4.7 copy-start.8
  272.9 4.6 copy-start.11
  277.6 2.0 copy-start.12
  290.5 4.3 copy-start.13
  303.0 285.7 %copy-start.1 = (bf16[1,4,10,128,128]{4,3,2,1,0:T(8,128)(2,1)S(1)}, bf16[1,4,10,128,128]{4,3,2,1,0:T(8,128)(2,1)}, u32[]{:S(2)}) copy-start(bf16[1,4,10,128,128]{4,3,2,1,0:T(8,128)(2,1)} %param.15) | copy-start | bytes 3932164
Sparse Core Ops, SparseCore 0:
  304.7 280.0 all-reduce.3
where the time goes:
time: 596 us
  waiting for transfers between devices  382 us (64%)
  blocking collectives  99.8 us (17%)
  local copies, waits for them, and re-layouts  33.8 us (6%)
  matrix products  24 us (4%)
  starting transfers between devices  22 us (4%)
  other arithmetic  19.7 us (3%)
  between operations  14.2 us (2%)
    all_to_all x2, waiting for transfers between devices, per_device(): lax.all_to_all(outgoing, 'dom', split_axis=0, concat_axis=0, tiled=True)  202 us
    psum x1, waiting for transfers between devices, per_device(): lax.psum((grad_w1, grad_b1, grad_w2, grad_b2), ('dp', 'dom'))  180 us
    psum x1, blocking collectives, per_device(): lax.psum((grad_w1, grad_b1, grad_w2, grad_b2), ('dp', 'dom'))  99.8 us
    all_to_all x2, starting transfers between devices, per_device(): lax.all_to_all(outgoing, 'dom', split_axis=0, concat_axis=0, tiled=True)  22 us
  transfers between devices with their start and end apart: 3, of which 3 were waited for; matrix products, arithmetic and copies ran while one was open for 0% of the time, Pallas kernels for 0%

commit v1 on v0

--- a/solution.py
+++ b/solution.py
@@ -87,7 +87,7 @@
         xbar, node_labels[0], labeled[0], weight_in, bias_in, weight_out, bias_out, scale
     )
     grad_w1, grad_b1, grad_w2, grad_b2 = lax.psum(
-        (grad_w1, grad_b1, grad_w2, grad_b2), ("dp", "dom")
+        lax.psum((grad_w1, grad_b1, grad_w2, grad_b2), "dp"), "dom"
     )
     return (grad_w1, grad_b1, grad_w2, grad_b2)
 

time: 596 us -> 731 us (1.23)
  the two profiles are of different devices: /device:TPU:17 before, /device:TPU:2 now
where the time goes in v1:
time: 731 us; the launch traced here: 730 us
  waiting for transfers between devices  521 us (71%)
  blocking collectives  97 us (13%)
  local copies, waits for them, and re-layouts  33.8 us (5%)
  matrix products  24 us (3%)
  starting transfers between devices  20.6 us (3%)
  other arithmetic  19.7 us (3%)
  between operations  14.2 us (2%)
    all_to_all x2, waiting for transfers between devices, per_device(): lax.all_to_all(outgoing, 'dom', split_axis=0, concat_axis=0, tiled=True)  204 us
    psum x1, waiting for transfers between devices, per_device(): lax.psum((grad_w1, grad_b1, grad_w2, grad_b2), 'dp')  175 us
    psum x1, waiting for transfers between devices, per_device(): lax.psum(lax.psum((grad_w1, grad_b1, grad_w2, grad_b2), 'dp'), 'dom')  142 us
    psum x1, blocking collectives, per_device(): lax.psum(lax.psum((grad_w1, grad_b1, grad_w2, grad_b2), 'dp'), 'dom')  54.7 us
    psum x1, blocking collectives, per_device(): lax.psum((grad_w1, grad_b1, grad_w2, grad_b2), 'dp')  42.3 us
    all_to_all x2, starting transfers between devices, per_device(): lax.all_to_all(outgoing, 'dom', split_axis=0, concat_axis=0, tiled=True)  20.5 us
  transfers between devices with their start and end apart: 4, of which 4 were waited for; matrix products, arithmetic and copies ran while one was open for 0% of the time, Pallas kernels for 0%

profile of v1, /device:TPU:2, one launch (start us, length us, event | category | flops | bytes accessed | tf_op | source)
XLA Modules:
  0.0 730.2 jit_solution(2296227216175438707)
XLA Ops:
  7.2 0.0 copy-start
  7.2 0.8 fusion.20
  8.0 1.2 broadcast_multiply_fusion
  9.2 3.1 gather_fusion
  12.3 12.0 %all-to-all-start = ((bf16[32,1,4,128,128]{4,3,2,1,0:T(8,128)(2,1)}), bf16[32,1,4,128,128]{4,3,2,1,0:T(8,128)(2,1)}, u32[]{:S(2)}, u32[]{:S(2)}) async-start(bf16[32,1,4,128,128]{4,3,2,1,0:T(8,128)(2,1)} %bitcast.86), calls=%async_computation | async-start | bytes 8388608 | tf_op jit(solution)/shard_map/all_to_all | solution.py:73
  24.3 0.1 reshape.132
  24.4 102.9 %all-to-all-done = bf16[32,1,4,128,128]{4,3,2,1,0:T(8,128)(2,1)} async-done(((bf16[32,1,4,128,128]{4,3,2,1,0:T(8,128)(2,1)}), bf16[32,1,4,128,128]{4,3,2,1,0:T(8,128)(2,1)}, u32[]{:S(2)}, u32[]{:S(2)}) %all-to-all-start) | async-done | bytes 4194336 | tf_op jit(solution)/shard_map/all_to_all | solution.py:73
  127.3 4.8 pad_maximum_fusion
  132.1 6.9 gather_fusion.1
  139.0 4.4 fusion.22
  143.4 3.1 gather_fusion.2
  146.5 8.5 %all-to-all-start.1 = ((bf16[32,1,4,128,128]{4,3,2,1,0:T(8,128)(2,1)}), bf16[32,1,4,128,128]{4,3,2,1,0:T(8,128)(2,1)}, u32[]{:S(2)}, u32[]{:S(2)}) async-start(bf16[32,1,4,128,128]{4,3,2,1,0:T(8,128)(2,1)} %bitcast.85), calls=%async_computation.1 | async-start | bytes 8388608 | tf_op jit(solution)/shard_map/all_to_all | solution.py:80
  155.0 0.0 all-reduce.9.cloned.1.call-start
  155.1 0.0 copy-done.5
  155.1 0.1 fusion.17
  155.2 0.2 sub.35
  155.4 1.7 sub.36
  157.2 100.9 %all-to-all-done.1 = bf16[32,1,4,128,128]{4,3,2,1,0:T(8,128)(2,1)} async-done(((bf16[32,1,4,128,128]{4,3,2,1,0:T(8,128)(2,1)}), bf16[32,1,4,128,128]{4,3,2,1,0:T(8,128)(2,1)}, u32[]{:S(2)}, u32[]{:S(2)}) %all-to-all-start.1) | async-done | bytes 4194336 | tf_op jit(solution)/shard_map/all_to_all | solution.py:80
  258.1 4.8 pad_maximum_fusion.1
  262.8 7.2 gather_fusion.3
  270.1 3.6 fusion.11
  273.6 0.0 copy-start.8
  273.7 0.0 copy-start.11
  273.7 4.6 multiply_convert_fusion
  278.3 1.6 fusion.23
  279.9 0.3 copy-done.12
  280.2 1.3 broadcast_divide_fusion
  281.5 3.0 reshape.121
  284.6 2.3 reduce_sum.55
  286.8 0.2 fusion.19
  287.0 0.1 fusion.18
  287.1 1.3 sub.38
  288.4 2.8 sub.39
  291.2 1.8 multiply_reduce_fusion
  293.0 2.5 fusion.21
  295.5 1.8 fusion.14
  297.3 6.5 fusion.24
  303.7 0.0 copy-start.1
  303.7 1.6 fusion
  305.3 0.0 all-reduce.9.cloned.1.call-update
  305.3 0.0 all-reduce.7.cloned.1.call-start
  305.4 174.9 %all-reduce.9.cloned.1.call-done = (f32[128,1024]{1,0:T(8,128)}, f32[1024,172]{0,1:T(8,128)}) async-done(((f32[128,1024]{1,0:T(8,128)}, f32[1024,172]{0,1:T(8,128)}), (f32[128,1024]{1,0:T(8,128)}, f32[1024,172]{0,1:T(8,128)})) %all-reduce.9.cloned.1.call-update) | async-done | bytes 1228816 | tf_op jit(solution)/shard_map/psum | solution.py:90
  480.3 0.0 all-reduce.7.cloned.1.call-update
  480.3 42.3 %all-reduce.2 = (f32[1024]{0:T(1024)S(1)}, f32[172]{0:T(256)S(1)}) all-reduce(f32[1024]{0:T(1024)S(1)} %get-tuple-element.20, f32[172]{0:T(256)S(1)} %get-tuple-element.12), channel_id=1, replica_groups=mesh['dp'=16,'dom'=32] {'dp'}, use_global_device_ids=true, to_apply=%region_7.8 | all-reduce | flops 1196 | bytes 9568 | tf_op jit(solution)/shard_map/psum | solution.py:90
  522.6 54.7 %all-reduce = (f32[1024]{0:T(1024)}, f32[172]{0:T(256)}) all-reduce(f32[1024]{0:T(1024)S(1)} %get-tuple-element.8, f32[172]{0:T(256)S(1)} %get-tuple-element.9), channel_id=1, replica_groups=mesh['dp'=16,'dom'=32] {'dom'}, use_global_device_ids=true, to_apply=%region_8.9 | all-reduce | flops 1196 | bytes 9568 | tf_op jit(solution)/shard_map/psum | solution.py:89
  577.3 142.2 %all-reduce.7.cloned.1.call-done = (f32[128,1024]{1,0:T(8,128)}, f32[1024,172]{0,1:T(8,128)}) async-done(((f32[128,1024]{1,0:T(8,128)}, f32[1024,172]{0,1:T(8,128)}), (f32[128,1024]{1,0:T(8,128)}, f32[1024,172]{0,1:T(8,128)})) %all-reduce.7.cloned.1.call-update) | async-done | bytes 1228816 | tf_op jit(solution)/shard_map/psum | solution.py:89
  719.5 1.9 copy.30
  721.3 2.0 copy.31
  (27 shorter events, 0.1 us)
Async XLA Ops:
  7.2 131.8 %copy-start = (bf16[1,4,10,128,128]{4,3,2,1,0:T(8,128)(2,1)S(1)}, bf16[1,4,10,128,128]{4,3,2,1,0:T(8,128)(2,1)}, u32[]{:S(2)}) copy-start(bf16[1,4,10,128,128]{4,3,2,1,0:T(8,128)(2,1)} %param.15) | copy-start | bytes 3932164
  12.3 12.0 %copy-start.6 = (s32[1,4,10]{2,1,0:T(4,128)S(1)}, s32[1,4,10]{2,1,0:T(4,128)}, u32[]{:S(2)}) copy-start(s32[1,4,10]{2,1,0:T(4,128)} %param.14) | copy-start | bytes 484
  12.3 115.0 %all-to-all-start = ((bf16[32,1,4,128,128]{4,3,2,1,0:T(8,128)(2,1)}), bf16[32,1,4,128,128]{4,3,2,1,0:T(8,128)(2,1)}, u32[]{:S(2)}, u32[]{:S(2)}) async-start(bf16[32,1,4,128,128]{4,3,2,1,0:T(8,128)(2,1)} %bitcast.86), calls=%async_computation | async-start | bytes 8388608 | tf_op jit(solution)/shard_map/all_to_all | solution.py:73
  146.5 8.6 %copy-start.7 = (s32[1,512]{1,0:T(1,128)S(1)}, s32[1,512]{1,0:T(1,128)}, u32[]{:S(2)}) copy-start(s32[1,512]{1,0:T(1,128)} %param.17) | copy-start | bytes 6148
  146.5 8.6 %copy-start.5 = (s32[1,512]{1,0:T(1,128)S(1)}, s32[1,512]{1,0:T(1,128)}, u32[]{:S(2)}) copy-start(s32[1,512]{1,0:T(1,128)} %param.16) | copy-start | bytes 6148
  146.5 111.6 %all-to-all-start.1 = ((bf16[32,1,4,128,128]{4,3,2,1,0:T(8,128)(2,1)}), bf16[32,1,4,128,128]{4,3,2,1,0:T(8,128)(2,1)}, u32[]{:S(2)}, u32[]{:S(2)}) async-start(bf16[32,1,4,128,128]{4,3,2,1,0:T(8,128)(2,1)} %bitcast.85), calls=%async_computation.1 | async-start | bytes 8388608 | tf_op jit(solution)/shard_map/all_to_all | solution.py:80
  155.0 325.3 %all-reduce.9.cloned.1.call-start = ((), (), s32[]{:S(2)}) async-start(), calls=%async_computation.3 | async-start | bytes 2490368 | tf_op jit(solution)/shard_map/psum | solution.py:90
  262.8 7.2 copy-start.2
  262.8 7.2 copy-start.3
  262.8 7.2 copy-start.4
  270.0 3.6 copy-start.9
  270.0 3.6 copy-start.10
  273.6 4.7 copy-start.8
  273.7 4.6 copy-start.11
  278.3 2.0 copy-start.12
  291.2 4.3 copy-start.13
  303.7 419.7 %copy-start.1 = (bf16[1,4,10,128,128]{4,3,2,1,0:T(8,128)(2,1)S(1)}, bf16[1,4,10,128,128]{4,3,2,1,0:T(8,128)(2,1)}, u32[]{:S(2)}) copy-start(bf16[1,4,10,128,128]{4,3,2,1,0:T(8,128)(2,1)} %param.15) | copy-start | bytes 3932164
  305.3 414.1 %all-reduce.7.cloned.1.call-start = ((), (), s32[]{:S(2)}) async-start(), calls=%async_computation.2 | async-start | bytes 2490368 | tf_op jit(solution)/shard_map/psum | solution.py:89
Sparse Core Ops, SparseCore 0:
  305.5 174.7 all-reduce.8
  483.3 236.1 all-reduce.6
